TPU v7x, 32 devices: a whole 2x2x4 slice. The times are simulated.
32 devices in a mesh: row: 8 (over z, x), col: 4 (over y, core).
Axes of the slice: x: 2, y: 2, z: 4, core: 2. Of those that a mesh axis runs over, the one named last changes fastest.
Arguments:
- right_side: float32 [6, 8, 64, 128], P(None, 'row'), may hold values from -6 to 6
- inverses: float32 [6, 8, 128, 128], P(None, 'row'), may hold values from -1 to 3
- factor_blocks: bfloat16 [15, 8, 8, 128, 128], P(None, 'row', 'col'), may hold values from -0.15625 to 0.15625
- pattern: int32 [15, 8, 8], P(None, 'row', 'col'), may hold values 0 or 1
Outputs:
- forward_part: float32 [6, 8, 64, 128], P(None, 'row')
- solution: float32 [6, 8, 64, 128], P(None, 'row')
All inputs are finite; a program needn't handle non-finite values. No bound on the sum of `pattern` on one device may be relied on, other than what follows from the above.
Results may differ from a plain program's by a relative error of at most 0.014.
Values may be sent and summed in bfloat16 or wider, within the bound.
No kernel may reach another device: no remote copies, remote signals or barrier semaphores. Data moves between devices by JAX's collectives and lax.ppermute only.
A program may use at most 64 MiB of HBM per device.

v0:
```python
import jax
import jax.numpy as jnp
from jax import lax
from jax.sharding import PartitionSpec as P


def spread(block, axis, holder):
    block = jnp.where(lax.axis_index(axis) == holder, block, jnp.zeros_like(block))
    return lax.psum(block, axis)


def pair_number(higher, lower_level):
    return higher * (higher - 1) // 2 + lower_level


def masked_block(factor_blocks, pattern, pair_index):
    return jnp.where(
        pattern[pair_index][:, :, None, None] != 0,
        factor_blocks[pair_index],
        jnp.zeros((), factor_blocks.dtype),
    )


def shards(right_side, inverses, factor_blocks, pattern):
    levels = right_side.shape[0]
    width_col = factor_blocks.shape[2]
    row_index = lax.axis_index("row")
    col_index = lax.axis_index("col")
    solved = []
    gathered = []
    for height in range(levels):
        remaining = right_side[height]
        if height > 0:
            partial_value = jnp.zeros(remaining.shape, jnp.float32)
            for earlier in range(height):
                masked = masked_block(factor_blocks, pattern, pair_number(height, earlier))
                partial_value = partial_value + jnp.einsum(
                    "ikab,knb->ina", masked, gathered[earlier], preferred_element_type=jnp.float32
                )
            summed = lax.psum(partial_value.astype(jnp.bfloat16), "col").astype(jnp.float32)
            remaining = remaining - summed
        segment = jnp.einsum(
            "inb,iab->ina", remaining, inverses[height], precision=lax.Precision.HIGHEST
        )
        solved.append(segment)
        if height < levels - 1:
            gathered_all = lax.all_gather(segment.astype(jnp.bfloat16), "row", axis=0, tiled=True)
            gathered.append(
                lax.dynamic_slice_in_dim(gathered_all, col_index * width_col, width_col, 0)
            )
    results = [None] * levels
    settled = [None] * levels
    for height in range(levels - 1, -1, -1):
        remaining = solved[height]
        if height < levels - 1:
            partial_value = jnp.zeros((width_col,) + remaining.shape[1:], jnp.float32)
            for later in range(height + 1, levels):
                masked = masked_block(factor_blocks, pattern, pair_number(later, height))
                partial_value = partial_value + jnp.einsum(
                    "ikab,ina->knb", masked, settled[later], preferred_element_type=jnp.float32
                )
            offset = jnp.clip(row_index - col_index * width_col, 0, width_col - 1)
            owner_col = row_index // width_col
            summed = lax.psum(partial_value, "row")
            own_sum = lax.dynamic_slice_in_dim(summed, offset, 1, 0)
            own_sum = spread(own_sum.astype(jnp.bfloat16), "col", owner_col).astype(own_sum.dtype)
            remaining = remaining - own_sum
        segment = jnp.einsum(
            "ina,iab->inb", remaining, inverses[height], precision=lax.Precision.HIGHEST
        )
        results[height] = segment
        settled[height] = segment.astype(jnp.bfloat16)
    return (jnp.stack(solved), jnp.stack(results))


def solution(mesh):
    placed = (
        P(None, "row", None, None),
        P(None, "row", None, None),
        P(None, "row", "col", None, None),
        P(None, "row", "col"),
    )
    return jax.shard_map(
        shards,
        mesh=mesh,
        in_specs=placed,
        out_specs=(P(None, "row", None, None), P(None, "row", None, None)),
        check_vma=False,
    )
```

profile of v0, /device:TPU:0, one launch (start us, length us, event | category | flops | bytes accessed | tf_op | source)
XLA Modules:
  0.0 446.8 jit_solution(956539431709333284)
XLA Ops:
  0.7 1.7 compare_reduce_fusion
  2.3 1.1 bitcast_dynamic-update-slice_fusion.10
  3.5 32.3 %all-gather = bf16[512,128]{1,0:T(8,128)(2,1)S(1)} all-gather(bf16[64,128]{1,0:T(8,128)(2,1)S(1)} %convert_element_type.125), channel_id=2, replica_groups=mesh['row'=8,'col'=4] {'row'}, dimensions={0}, use_global_device_ids=true | all-gather | bytes 147456 | tf_op jit(solution)/shard_map/all_gather | solution.py:47
  35.8 1.0 fusion.24
  36.8 10.1 %psum.105 = bf16[1,64,128]{2,1,0:T(8,128)(2,1)S(1)} all-reduce(bf16[1,64,128]{2,1,0:T(8,128)(2,1)S(1)} %fusion.24), channel_id=1, replica_groups=mesh['row'=8,'col'=4] {'col'}, use_global_device_ids=true, to_apply=%region_0.1 | all-reduce | flops 8192 | bytes 32768 | tf_op jit(solution)/shard_map/psum | solution.py:40
  47.0 1.1 bitcast_dynamic-update-slice_fusion.9
  48.1 1.0 convolution_bitcast_fusion.15
  49.8 30.7 %all-gather.1 = bf16[512,128]{1,0:T(8,128)(2,1)S(1)} all-gather(bf16[64,128]{1,0:T(8,128)(2,1)S(1)} %convert_element_type.130), channel_id=3, replica_groups=mesh['row'=8,'col'=4] {'row'}, dimensions={0}, use_global_device_ids=true | all-gather | bytes 147456 | tf_op jit(solution)/shard_map/all_gather | solution.py:47
  80.7 10.1 %psum.106 = bf16[1,64,128]{2,1,0:T(8,128)(2,1)S(1)} all-reduce(bf16[1,64,128]{2,1,0:T(8,128)(2,1)S(1)} %fusion.23), channel_id=1, replica_groups=mesh['row'=8,'col'=4] {'col'}, use_global_device_ids=true, to_apply=%region_1.2 | all-reduce | flops 8192 | bytes 32768 | tf_op jit(solution)/shard_map/psum | solution.py:40
  91.3 0.2 fusion.8
  91.5 0.5 copy-done.2
  92.0 0.2 bitcast_dynamic-update-slice_fusion.8
  92.2 30.5 %all-gather.2 = bf16[512,128]{1,0:T(8,128)(2,1)S(1)} all-gather(bf16[64,128]{1,0:T(8,128)(2,1)S(1)} %convert_element_type.135), channel_id=4, replica_groups=mesh['row'=8,'col'=4] {'row'}, dimensions={0}, use_global_device_ids=true | all-gather | bytes 147456 | tf_op jit(solution)/shard_map/all_gather | solution.py:47
  123.0 10.1 %psum.107 = bf16[1,64,128]{2,1,0:T(8,128)(2,1)S(1)} all-reduce(bf16[1,64,128]{2,1,0:T(8,128)(2,1)S(1)} %fusion.22), channel_id=1, replica_groups=mesh['row'=8,'col'=4] {'col'}, use_global_device_ids=true, to_apply=%region_2.3 | all-reduce | flops 8192 | bytes 32768 | tf_op jit(solution)/shard_map/psum | solution.py:40
  133.5 0.3 bitcast_dynamic-update-slice_fusion.7
  133.8 30.5 %all-gather.3 = bf16[512,128]{1,0:T(8,128)(2,1)S(1)} all-gather(bf16[64,128]{1,0:T(8,128)(2,1)S(1)} %convert_element_type.140), channel_id=5, replica_groups=mesh['row'=8,'col'=4] {'row'}, dimensions={0}, use_global_device_ids=true | all-gather | bytes 147456 | tf_op jit(solution)/shard_map/all_gather | solution.py:47
  164.8 10.1 %psum.108 = bf16[1,64,128]{2,1,0:T(8,128)(2,1)S(1)} all-reduce(bf16[1,64,128]{2,1,0:T(8,128)(2,1)S(1)} %fusion.21), channel_id=1, replica_groups=mesh['row'=8,'col'=4] {'col'}, use_global_device_ids=true, to_apply=%region_3.4 | all-reduce | flops 8192 | bytes 32768 | tf_op jit(solution)/shard_map/psum | solution.py:40
  174.9 0.2 bitcast_dynamic-update-slice_fusion.6
  175.2 30.5 %all-gather.4 = bf16[512,128]{1,0:T(8,128)(2,1)S(1)} all-gather(bf16[64,128]{1,0:T(8,128)(2,1)S(1)} %convert_element_type.145), channel_id=6, replica_groups=mesh['row'=8,'col'=4] {'row'}, dimensions={0}, use_global_device_ids=true | all-gather | bytes 147456 | tf_op jit(solution)/shard_map/all_gather | solution.py:47
  205.9 10.1 %psum.109 = bf16[1,64,128]{2,1,0:T(8,128)(2,1)S(1)} all-reduce(bf16[1,64,128]{2,1,0:T(8,128)(2,1)S(1)} %fusion.20), channel_id=1, replica_groups=mesh['row'=8,'col'=4] {'col'}, use_global_device_ids=true, to_apply=%region_4.5 | all-reduce | flops 8192 | bytes 32768 | tf_op jit(solution)/shard_map/psum | solution.py:40
  216.0 0.2 bitcast_dynamic-update-slice_fusion.5
  216.7 37.5 %psum.110 = bf16[2,64,128]{2,1,0:T(8,128)(2,1)S(1)} all-reduce(f32[2,64,128]{2,1,0:T(8,128)S(1)} %convolution_bitcast_fusion), channel_id=1, replica_groups=mesh['row'=8,'col'=4] {'row'}, use_global_device_ids=true, to_apply=%region_5.6 | all-reduce | flops 16384 | bytes 98304 | tf_op jit(solution)/shard_map/psum | solution.py:64
  254.2 10.1 %psum.111 = bf16[1,64,128]{2,1,0:T(8,128)(2,1)S(1)} all-reduce(bf16[1,64,128]{2,1,0:T(8,128)(2,1)S(1)} %fusion.221), channel_id=1, replica_groups=mesh['row'=8,'col'=4] {'col'}, use_global_device_ids=true, to_apply=%region_6.7 | all-reduce | flops 8192 | bytes 32768 | tf_op jit(solution)/shard_map/psum | solution.py:9
  264.9 33.4 %psum.112 = bf16[2,64,128]{2,1,0:T(8,128)(2,1)S(1)} all-reduce(f32[2,64,128]{2,1,0:T(8,128)S(1)} %fusion.3), channel_id=1, replica_groups=mesh['row'=8,'col'=4] {'row'}, use_global_device_ids=true, to_apply=%region_7.8 | all-reduce | flops 16384 | bytes 98304 | tf_op jit(solution)/shard_map/psum | solution.py:64
  298.3 10.1 %psum.113 = bf16[1,64,128]{2,1,0:T(8,128)(2,1)S(1)} all-reduce(bf16[1,64,128]{2,1,0:T(8,128)(2,1)S(1)} %fusion.222), channel_id=1, replica_groups=mesh['row'=8,'col'=4] {'col'}, use_global_device_ids=true, to_apply=%region_8.9 | all-reduce | flops 8192 | bytes 32768 | tf_op jit(solution)/shard_map/psum | solution.py:9
  309.2 35.3 %psum.114 = bf16[2,64,128]{2,1,0:T(8,128)(2,1)S(1)} all-reduce(f32[2,64,128]{2,1,0:T(8,128)S(1)} %fusion.2), channel_id=1, replica_groups=mesh['row'=8,'col'=4] {'row'}, use_global_device_ids=true, to_apply=%region_9.10 | all-reduce | flops 16384 | bytes 98304 | tf_op jit(solution)/shard_map/psum | solution.py:64
  344.6 10.1 %psum.115 = bf16[1,64,128]{2,1,0:T(8,128)(2,1)S(1)} all-reduce(bf16[1,64,128]{2,1,0:T(8,128)(2,1)S(1)} %fusion.223), channel_id=1, replica_groups=mesh['row'=8,'col'=4] {'col'}, use_global_device_ids=true, to_apply=%region_10.11 | all-reduce | flops 8192 | bytes 32768 | tf_op jit(solution)/shard_map/psum | solution.py:9
  355.7 33.4 %psum.116 = bf16[2,64,128]{2,1,0:T(8,128)(2,1)S(1)} all-reduce(f32[2,64,128]{2,1,0:T(8,128)S(1)} %fusion.1), channel_id=1, replica_groups=mesh['row'=8,'col'=4] {'row'}, use_global_device_ids=true, to_apply=%region_11.12 | all-reduce | flops 16384 | bytes 98304 | tf_op jit(solution)/shard_map/psum | solution.py:64
  389.1 10.1 %psum.117 = bf16[1,64,128]{2,1,0:T(8,128)(2,1)S(1)} all-reduce(bf16[1,64,128]{2,1,0:T(8,128)(2,1)S(1)} %fusion.224), channel_id=1, replica_groups=mesh['row'=8,'col'=4] {'col'}, use_global_device_ids=true, to_apply=%region_12.13 | all-reduce | flops 8192 | bytes 32768 | tf_op jit(solution)/shard_map/psum | solution.py:9
  400.4 35.3 %psum.118 = bf16[2,64,128]{2,1,0:T(8,128)(2,1)S(1)} all-reduce(f32[2,64,128]{2,1,0:T(8,128)S(1)} %fusion), channel_id=1, replica_groups=mesh['row'=8,'col'=4] {'row'}, use_global_device_ids=true, to_apply=%region_13.14 | all-reduce | flops 16384 | bytes 98304 | tf_op jit(solution)/shard_map/psum | solution.py:64
  435.8 10.1 %psum.119 = bf16[1,64,128]{2,1,0:T(8,128)(2,1)S(1)} all-reduce(bf16[1,64,128]{2,1,0:T(8,128)(2,1)S(1)} %fusion.225), channel_id=1, replica_groups=mesh['row'=8,'col'=4] {'col'}, use_global_device_ids=true, to_apply=%region_14.15 | all-reduce | flops 8192 | bytes 32768 | tf_op jit(solution)/shard_map/psum | solution.py:9
  446.2 0.7 copy-done.4
  (56 shorter events, 6.8 us)
Async XLA Ops:
  0.6 48.5 %copy-start = (bf16[15,1,2,128,128]{4,3,2,1,0:T(8,128)(2,1)S(1)}, bf16[15,1,2,128,128]{4,3,2,1,0:T(8,128)(2,1)}, u32[]{:S(2)}) copy-start(bf16[15,1,2,128,128]{4,3,2,1,0:T(8,128)(2,1)} %param.6) | copy-start | bytes 2949124
  49.8 41.7 %copy-start.1 = (f32[6,1,128,128]{3,2,1,0:T(8,128)S(1)}, f32[6,1,128,128]{3,2,1,0:T(8,128)}, u32[]{:S(2)}) copy-start(f32[6,1,128,128]{3,2,1,0:T(8,128)} %param.5) | copy-start | bytes 1179652
  91.0 1.0 copy-start.2
  216.3 37.9 %copy-start.3 = (f32[6,1,64,128]{3,2,1,0:T(8,128)}, f32[6,1,64,128]{3,2,1,0:T(8,128)S(1)}, u32[]{:S(2)}) copy-start(f32[6,1,64,128]{3,2,1,0:T(8,128)S(1)} %get-tuple-element.27) | copy-start | bytes 589828
  446.1 0.7 copy-start.4
where the time goes:
time: 448 us; the launch traced here: 447 us
  blocking collectives  431 us (96%)
  matrix products  12.2 us (3%)
    psum x5, blocking collectives, shards(): summed = lax.psum(partial_value, 'row')  175 us
    all_gather x5, blocking collectives, shards(): lax.all_gather(segment.astype(jnp.bfloat16), 'row', axis=0, tiled=True)  155 us
    psum x5, blocking collectives, shards(): lax.psum(partial_value.astype(jnp.bfloat16), 'col').astype(jnp.float32)  50.7 us
    psum x5, blocking collectives, spread(): return lax.psum(block, axis)  50.6 us

commit v1 on v0

--- a/solution.py
+++ b/solution.py
@@ -44,7 +44,12 @@
         )
         solved.append(segment)
         if height < levels - 1:
-            gathered_all = lax.all_gather(segment.astype(jnp.bfloat16), "row", axis=0, tiled=True)
+            gathered_all = jnp.concatenate(
+                lax.all_to_all(
+                    jnp.stack([segment.astype(jnp.bfloat16)] * lax.axis_size("row")), "row", 0, 0
+                ),
+                axis=0,
+            )
             gathered.append(
                 lax.dynamic_slice_in_dim(gathered_all, col_index * width_col, width_col, 0)
             )

time: 448 us -> 346 us (0.77)
  blocking collectives: 431 us -> 273 us
  waiting for transfers between devices: 0 us -> 32.6 us
  starting transfers between devices: 0 us -> 20.8 us
    all_gather x5 -> x0, blocking collectives: 155 us -> none  [shards(): lax.all_gather(segment.astype(jnp.bfloat16), 'row', axis=0, tiled=True)]
    all_to_all x0 -> x5, waiting for transfers between devices: none -> 32.6 us  [shards(): lax.all_to_all(jnp.stack([segment.astype(jnp.bfloat16)] * lax.axis_size('...]
    all_to_all x0 -> x5, starting transfers between devices: none -> 20.8 us  [shards(): lax.all_to_all(jnp.stack([segment.astype(jnp.bfloat16)] * lax.axis_size('...]
  transfers between devices with their start and end apart: 0 -> 5, of which waited for: 0 -> 5; matrix products, arithmetic and copies ran while one was open for 0% -> 1% of each run, Pallas kernels for 0% -> 0%
where the time goes in v1:
time: 346 us; the launch traced here: 345 us
  blocking collectives  273 us (79%)
  waiting for transfers between devices  32.6 us (9%)
  starting transfers between devices  20.8 us (6%)
  matrix products  11.3 us (3%)
  local copies, waits for them, and re-layouts  4.08 us (1%)
    psum x5, blocking collectives, shards(): summed = lax.psum(partial_value, 'row')  172 us
    psum x5, blocking collectives, shards(): lax.psum(partial_value.astype(jnp.bfloat16), 'col').astype(jnp.float32)  50.7 us
    psum x5, blocking collectives, spread(): return lax.psum(block, axis)  50.6 us
    all_to_all x5, waiting for transfers between devices, shards(): lax.all_to_all(jnp.stack([segment.astype(jnp.bfloat16)] * lax.axis_size('...  32.6 us
    all_to_all x5, starting transfers between devices, shards(): lax.all_to_all(jnp.stack([segment.astype(jnp.bfloat16)] * lax.axis_size('...  20.8 us
  transfers between devices with their start and end apart: 5, of which 5 were waited for; matrix products, arithmetic and copies ran while one was open for 1% of the time, Pallas kernels for 0%

profile of v1, /device:TPU:0, one launch (start us, length us, event | category | flops | bytes accessed | tf_op | source)
XLA Modules:
  0.0 344.9 jit_solution(7649832478856620124)
XLA Ops:
  0.7 1.2 bitcast_dynamic-update-slice_fusion.10
  1.9 0.7 stack.39
  2.5 7.3 %all-to-all-start = ((bf16[8,1,64,128]{3,2,1,0:T(8,128)(2,1)}), bf16[8,1,64,128]{3,2,1,0:T(8,128)(2,1)S(1)}, u32[]{:S(2)}, u32[]{:S(2)}) async-start(bf16[8,1,64,128]{3,2,1,0:T(8,128)(2,1)} %stack.39), calls=%async_computation | async-start | bytes 262144 | tf_op jit(solution)/shard_map/all_to_all | solution.py:48
  9.8 1.7 compare_reduce_fusion
  11.5 5.7 %all-to-all-done = bf16[8,1,64,128]{3,2,1,0:T(8,128)(2,1)S(1)} async-done(((bf16[8,1,64,128]{3,2,1,0:T(8,128)(2,1)}), bf16[8,1,64,128]{3,2,1,0:T(8,128)(2,1)S(1)}, u32[]{:S(2)}, u32[]{:S(2)}) %all-to-all-start) | async-done | bytes 131104 | tf_op jit(solution)/shard_map/all_to_all | solution.py:48
  17.2 1.0 fusion.24
  18.2 10.1 %psum.105 = bf16[1,64,128]{2,1,0:T(8,128)(2,1)S(1)} all-reduce(bf16[1,64,128]{2,1,0:T(8,128)(2,1)S(1)} %fusion.24), channel_id=1, replica_groups=mesh['row'=8,'col'=4] {'col'}, use_global_device_ids=true, to_apply=%region_0.1 | all-reduce | flops 8192 | bytes 32768 | tf_op jit(solution)/shard_map/psum | solution.py:40
  28.3 1.0 bitcast_dynamic-update-slice_fusion.9
  29.4 0.7 stack.41
  30.0 3.4 all-to-all-start.1
  34.3 6.4 %all-to-all-done.1 = bf16[8,1,64,128]{3,2,1,0:T(8,128)(2,1)S(1)} async-done(((bf16[8,1,64,128]{3,2,1,0:T(8,128)(2,1)}), bf16[8,1,64,128]{3,2,1,0:T(8,128)(2,1)S(1)}, u32[]{:S(2)}, u32[]{:S(2)}) %all-to-all-start.1) | async-done | bytes 131104 | tf_op jit(solution)/shard_map/all_to_all | solution.py:48
  40.9 10.1 %psum.106 = bf16[1,64,128]{2,1,0:T(8,128)(2,1)S(1)} all-reduce(bf16[1,64,128]{2,1,0:T(8,128)(2,1)S(1)} %fusion.23), channel_id=1, replica_groups=mesh['row'=8,'col'=4] {'col'}, use_global_device_ids=true, to_apply=%region_1.2 | all-reduce | flops 8192 | bytes 32768 | tf_op jit(solution)/shard_map/psum | solution.py:40
  51.3 0.7 stack.43
  52.0 3.4 all-to-all-start.2
  55.8 6.9 %all-to-all-done.2 = bf16[8,1,64,128]{3,2,1,0:T(8,128)(2,1)S(1)} async-done(((bf16[8,1,64,128]{3,2,1,0:T(8,128)(2,1)}), bf16[8,1,64,128]{3,2,1,0:T(8,128)(2,1)S(1)}, u32[]{:S(2)}, u32[]{:S(2)}) %all-to-all-start.2) | async-done | bytes 131104 | tf_op jit(solution)/shard_map/all_to_all | solution.py:48
  62.8 10.1 %psum.107 = bf16[1,64,128]{2,1,0:T(8,128)(2,1)S(1)} all-reduce(bf16[1,64,128]{2,1,0:T(8,128)(2,1)S(1)} %fusion.22), channel_id=1, replica_groups=mesh['row'=8,'col'=4] {'col'}, use_global_device_ids=true, to_apply=%region_2.3 | all-reduce | flops 8192 | bytes 32768 | tf_op jit(solution)/shard_map/psum | solution.py:40
  73.9 3.4 all-to-all-start.3
  77.7 6.9 %all-to-all-done.3 = bf16[8,1,64,128]{3,2,1,0:T(8,128)(2,1)S(1)} async-done(((bf16[8,1,64,128]{3,2,1,0:T(8,128)(2,1)}), bf16[8,1,64,128]{3,2,1,0:T(8,128)(2,1)S(1)}, u32[]{:S(2)}, u32[]{:S(2)}) %all-to-all-start.3) | async-done | bytes 131104 | tf_op jit(solution)/shard_map/all_to_all | solution.py:48
  84.8 10.1 %psum.108 = bf16[1,64,128]{2,1,0:T(8,128)(2,1)S(1)} all-reduce(bf16[1,64,128]{2,1,0:T(8,128)(2,1)S(1)} %fusion.21), channel_id=1, replica_groups=mesh['row'=8,'col'=4] {'col'}, use_global_device_ids=true, to_apply=%region_3.4 | all-reduce | flops 8192 | bytes 32768 | tf_op jit(solution)/shard_map/psum | solution.py:40
  95.8 3.4 all-to-all-start.4
  99.6 6.9 %all-to-all-done.4 = bf16[8,1,64,128]{3,2,1,0:T(8,128)(2,1)S(1)} async-done(((bf16[8,1,64,128]{3,2,1,0:T(8,128)(2,1)}), bf16[8,1,64,128]{3,2,1,0:T(8,128)(2,1)S(1)}, u32[]{:S(2)}, u32[]{:S(2)}) %all-to-all-start.4) | async-done | bytes 131104 | tf_op jit(solution)/shard_map/all_to_all | solution.py:48
  106.7 10.1 %psum.109 = bf16[1,64,128]{2,1,0:T(8,128)(2,1)S(1)} all-reduce(bf16[1,64,128]{2,1,0:T(8,128)(2,1)S(1)} %fusion.20), channel_id=1, replica_groups=mesh['row'=8,'col'=4] {'col'}, use_global_device_ids=true, to_apply=%region_4.5 | all-reduce | flops 8192 | bytes 32768 | tf_op jit(solution)/shard_map/psum | solution.py:40
  117.5 34.4 %psum.110 = bf16[2,64,128]{2,1,0:T(8,128)(2,1)S(1)} all-reduce(f32[2,64,128]{2,1,0:T(8,128)S(1)} %convolution_bitcast_fusion), channel_id=1, replica_groups=mesh['row'=8,'col'=4] {'row'}, use_global_device_ids=true, to_apply=%region_5.6 | all-reduce | flops 16384 | bytes 98304 | tf_op jit(solution)/shard_map/psum | solution.py:69
  152.0 10.1 %psum.111 = bf16[1,64,128]{2,1,0:T(8,128)(2,1)S(1)} all-reduce(bf16[1,64,128]{2,1,0:T(8,128)(2,1)S(1)} %fusion.236), channel_id=1, replica_groups=mesh['row'=8,'col'=4] {'col'}, use_global_device_ids=true, to_apply=%region_6.7 | all-reduce | flops 8192 | bytes 32768 | tf_op jit(solution)/shard_map/psum | solution.py:9
  162.7 34.4 %psum.112 = bf16[2,64,128]{2,1,0:T(8,128)(2,1)S(1)} all-reduce(f32[2,64,128]{2,1,0:T(8,128)S(1)} %fusion.3), channel_id=1, replica_groups=mesh['row'=8,'col'=4] {'row'}, use_global_device_ids=true, to_apply=%region_7.8 | all-reduce | flops 16384 | bytes 98304 | tf_op jit(solution)/shard_map/psum | solution.py:69
  197.1 10.1 %psum.113 = bf16[1,64,128]{2,1,0:T(8,128)(2,1)S(1)} all-reduce(bf16[1,64,128]{2,1,0:T(8,128)(2,1)S(1)} %fusion.237), channel_id=1, replica_groups=mesh['row'=8,'col'=4] {'col'}, use_global_device_ids=true, to_apply=%region_8.9 | all-reduce | flops 8192 | bytes 32768 | tf_op jit(solution)/shard_map/psum | solution.py:9
  208.0 34.4 %psum.114 = bf16[2,64,128]{2,1,0:T(8,128)(2,1)S(1)} all-reduce(f32[2,64,128]{2,1,0:T(8,128)S(1)} %fusion.2), channel_id=1, replica_groups=mesh['row'=8,'col'=4] {'row'}, use_global_device_ids=true, to_apply=%region_9.10 | all-reduce | flops 16384 | bytes 98304 | tf_op jit(solution)/shard_map/psum | solution.py:69
  242.5 10.1 %psum.115 = bf16[1,64,128]{2,1,0:T(8,128)(2,1)S(1)} all-reduce(bf16[1,64,128]{2,1,0:T(8,128)(2,1)S(1)} %fusion.238), channel_id=1, replica_groups=mesh['row'=8,'col'=4] {'col'}, use_global_device_ids=true, to_apply=%region_10.11 | all-reduce | flops 8192 | bytes 32768 | tf_op jit(solution)/shard_map/psum | solution.py:9
  253.6 34.4 %psum.116 = bf16[2,64,128]{2,1,0:T(8,128)(2,1)S(1)} all-reduce(f32[2,64,128]{2,1,0:T(8,128)S(1)} %fusion.1), channel_id=1, replica_groups=mesh['row'=8,'col'=4] {'row'}, use_global_device_ids=true, to_apply=%region_11.12 | all-reduce | flops 16384 | bytes 98304 | tf_op jit(solution)/shard_map/psum | solution.py:69
  288.0 10.1 %psum.117 = bf16[1,64,128]{2,1,0:T(8,128)(2,1)S(1)} all-reduce(bf16[1,64,128]{2,1,0:T(8,128)(2,1)S(1)} %fusion.239), channel_id=1, replica_groups=mesh['row'=8,'col'=4] {'col'}, use_global_device_ids=true, to_apply=%region_12.13 | all-reduce | flops 8192 | bytes 32768 | tf_op jit(solution)/shard_map/psum | solution.py:9
  299.4 34.4 %psum.118 = bf16[2,64,128]{2,1,0:T(8,128)(2,1)S(1)} all-reduce(f32[2,64,128]{2,1,0:T(8,128)S(1)} %fusion), channel_id=1, replica_groups=mesh['row'=8,'col'=4] {'row'}, use_global_device_ids=true, to_apply=%region_13.14 | all-reduce | flops 16384 | bytes 98304 | tf_op jit(solution)/shard_map/psum | solution.py:69
  333.8 10.1 %psum.119 = bf16[1,64,128]{2,1,0:T(8,128)(2,1)S(1)} all-reduce(bf16[1,64,128]{2,1,0:T(8,128)(2,1)S(1)} %fusion.240), channel_id=1, replica_groups=mesh['row'=8,'col'=4] {'col'}, use_global_device_ids=true, to_apply=%region_14.15 | all-reduce | flops 8192 | bytes 32768 | tf_op jit(solution)/shard_map/psum | solution.py:9
  (66 shorter events, 10.2 us)
Async XLA Ops:
  0.6 27.7 %copy-start.1 = (f32[6,1,128,128]{3,2,1,0:T(8,128)S(1)}, f32[6,1,128,128]{3,2,1,0:T(8,128)}, u32[]{:S(2)}) copy-start(f32[6,1,128,128]{3,2,1,0:T(8,128)} %param.5) | copy-start | bytes 1179652
  0.6 32.8 %copy-start = (bf16[15,1,2,128,128]{4,3,2,1,0:T(8,128)(2,1)S(1)}, bf16[15,1,2,128,128]{4,3,2,1,0:T(8,128)(2,1)}, u32[]{:S(2)}) copy-start(bf16[15,1,2,128,128]{4,3,2,1,0:T(8,128)(2,1)} %param.6) | copy-start | bytes 2949124
  2.5 14.6 %all-to-all-start = ((bf16[8,1,64,128]{3,2,1,0:T(8,128)(2,1)}), bf16[8,1,64,128]{3,2,1,0:T(8,128)(2,1)S(1)}, u32[]{:S(2)}, u32[]{:S(2)}) async-start(bf16[8,1,64,128]{3,2,1,0:T(8,128)(2,1)} %stack.39), calls=%async_computation | async-start | bytes 262144 | tf_op jit(solution)/shard_map/all_to_all | solution.py:48
  30.0 10.7 %all-to-all-start.1 = ((bf16[8,1,64,128]{3,2,1,0:T(8,128)(2,1)}), bf16[8,1,64,128]{3,2,1,0:T(8,128)(2,1)S(1)}, u32[]{:S(2)}, u32[]{:S(2)}) async-start(bf16[8,1,64,128]{3,2,1,0:T(8,128)(2,1)} %stack.41), calls=%async_computation.1 | async-start | bytes 262144 | tf_op jit(solution)/shard_map/all_to_all | solution.py:48
  34.1 17.0 %copy-start.2 = (f32[6,1,64,128]{3,2,1,0:T(8,128)S(1)}, f32[6,1,64,128]{3,2,1,0:T(8,128)}, u32[]{:S(2)}) copy-start(f32[6,1,64,128]{3,2,1,0:T(8,128)} %param.4) | copy-start | bytes 589828
  52.0 10.7 %all-to-all-start.2 = ((bf16[8,1,64,128]{3,2,1,0:T(8,128)(2,1)}), bf16[8,1,64,128]{3,2,1,0:T(8,128)(2,1)S(1)}, u32[]{:S(2)}, u32[]{:S(2)}) async-start(bf16[8,1,64,128]{3,2,1,0:T(8,128)(2,1)} %stack.43), calls=%async_computation.2 | async-start | bytes 262144 | tf_op jit(solution)/shard_map/all_to_all | solution.py:48
  73.9 10.7 %all-to-all-start.3 = ((bf16[8,1,64,128]{3,2,1,0:T(8,128)(2,1)}), bf16[8,1,64,128]{3,2,1,0:T(8,128)(2,1)S(1)}, u32[]{:S(2)}, u32[]{:S(2)}) async-start(bf16[8,1,64,128]{3,2,1,0:T(8,128)(2,1)} %stack.45), calls=%async_computation.3 | async-start | bytes 262144 | tf_op jit(solution)/shard_map/all_to_all | solution.py:48
  95.8 10.7 %all-to-all-start.4 = ((bf16[8,1,64,128]{3,2,1,0:T(8,128)(2,1)}), bf16[8,1,64,128]{3,2,1,0:T(8,128)(2,1)S(1)}, u32[]{:S(2)}, u32[]{:S(2)}) async-start(bf16[8,1,64,128]{3,2,1,0:T(8,128)(2,1)} %stack.47), calls=%async_computation.4 | async-start | bytes 262144 | tf_op jit(solution)/shard_map/all_to_all | solution.py:48
  117.1 34.9 %copy-start.3 = (f32[6,1,64,128]{3,2,1,0:T(8,128)}, f32[6,1,64,128]{3,2,1,0:T(8,128)S(1)}, u32[]{:S(2)}) copy-start(f32[6,1,64,128]{3,2,1,0:T(8,128)S(1)} %get-tuple-element.27) | copy-start | bytes 589828
  344.2 0.7 copy-start.4
